TPU v7x, 256 devices: a whole 4x4x8 slice. The times are simulated.
256 devices in a mesh: seq: 32 (over x, y, core), head: 8 (over z).
Axes of the slice: x: 4, y: 4, z: 8, core: 2. Of those that a mesh axis runs over, the one named last changes fastest.
Arguments:
- new_states: bfloat16 [96, 1024], replicated, may hold values from -6 to 6
- lengths: int32 [24], replicated, may hold values from 1 to 16380, as said below
- cache_keys: bfloat16 [24, 16384, 1024], P(None, 'seq', 'head'), may hold values from -3000 to 3000
- cache_values: bfloat16 [24, 16384, 1024], P(None, 'seq', 'head'), may hold values from -6 to 6
- buckets: int32 [24, 4, 16384], P(None, None, 'seq'), may hold values from 0 to 31, as said below
- attn_gain: float32 [1024], replicated, may hold values from 0.25 to 1.75
- w_query: bfloat16 [1024, 1024], P(None, 'head'), may hold values from -0.0234375 to 0.0234375
- w_key: bfloat16 [1024, 1024], P(None, 'head'), may hold values from -0.1875 to 0.1875
- w_value: bfloat16 [1024, 1024], P(None, 'head'), may hold values from -0.1875 to 0.1875
- rel_bias: float32 [32, 16], P(None, 'head'), may hold values from -27 to 2
- w_out: bfloat16 [1024, 1024], P('head'), may hold values from -0.1875 to 0.1875
- ffn_gain: float32 [1024], replicated, may hold values from 0.25 to 1.75
- w_router: float32 [1024, 16], replicated, may hold values from -0.1875 to 0.1875
- w_gate: bfloat16 [16, 1024, 2816], P('head', None, 'seq'), may hold values from -0.1875 to 0.1875
- w_up: bfloat16 [16, 1024, 2816], P('head', None, 'seq'), may hold values from -0.1875 to 0.1875
- w_down: bfloat16 [16, 2816, 1024], P('head', 'seq'), may hold values from -0.109375 to 0.109375
- expert_picks: int32 [4, 24, 2], replicated, may hold values from 0 to 15, all different within a row; in each aligned block of 24 rows (0 to 23, 24 to 47, ..., all dimensions but the last counted through in order) at most 4 rows name the same one
- final_gain: float32 [1024], replicated, may hold values from 0.25 to 1.75
- w_vocab: bfloat16 [1024, 32128], P(None, 'seq'), may hold values from -0.5 to 0.5
Outputs:
- final_hidden: bfloat16 [96, 1024], P('head')
- hidden_norm: float32 [96], P('head')
- logit_max: float32 [96], P('head')
Inputs may be any that keep to these rules, and one draw needn't show every extreme that they name: `lengths`: some request has exactly 16380 cached positions. buckets[r, t, p] is the T5 relative position bucket (16 exact buckets, then logarithmic up to a distance of 128) of the distance lengths[r] + t - p where that is not negative, else 0. `expert_picks`: A request's two picks at a step differ; at each step no expert is picked by more than 4 requests, a bound that some block reaches.
All inputs are finite; a program needn't handle non-finite values.
Results may differ from a plain program's by a relative error of at most 0.0096.
Values may be sent and summed in bfloat16 or wider, within the bound.
A program may use at most 64 MiB of HBM per device.

v0:
```python
import jax
import jax.numpy as jnp
from jax import lax
from jax.sharding import PartitionSpec as P

CAP = 4


def joined(part, axis, combine):
    gathered = jax.tree.map(lambda a: lax.all_gather(a, axis), part)

    def take(source):
        return jax.tree.map(lambda a: lax.dynamic_index_in_dim(a, source, 0, False), gathered)

    return lax.fori_loop(
        1, lax.axis_size(axis), lambda source, state: combine(state, take(source)), take(0)
    )


def norm_parts(values, gain_row):
    norm_root = jnp.sqrt(jnp.mean(values * values, axis=-1, keepdims=True) + 1e-06)
    return (values / norm_root * gain_row, norm_root[..., 0])


def join_three(earlier_part, later_part):
    joint_top = jnp.maximum(earlier_part[0], later_part[0])
    lead_scale = jnp.exp(earlier_part[0] - joint_top)
    trail_scale = jnp.exp(later_part[0] - joint_top)
    mass = earlier_part[1] * lead_scale + later_part[1] * trail_scale
    weighted = earlier_part[2] * lead_scale[..., None] + later_part[2] * trail_scale[..., None]
    return (joint_top, mass, weighted)


def shards(
    new_states,
    lengths,
    cache_keys,
    cache_values,
    buckets,
    attn_gain,
    w_query,
    w_key,
    w_value,
    rel_bias,
    w_out,
    ffn_gain,
    w_router,
    w_gate,
    w_up,
    w_down,
    expert_picks,
    final_gain,
    w_vocab,
):
    seq_count = lax.axis_size("seq")
    head_count = lax.axis_size("head")
    seq_index = lax.axis_index("seq")
    head_index = lax.axis_index("head")
    requests, span_local, inner_local = cache_keys.shape
    tokens = new_states.shape[0]
    step_count = tokens // requests
    bucket_count, heads_local = rel_bias.shape
    head_dim = inner_local // heads_local
    states = new_states.astype(jnp.float32)
    scaled, _ = norm_parts(states, attn_gain)
    scaled = scaled.astype(jnp.bfloat16)
    queries = (
        jnp.dot(scaled, w_query, preferred_element_type=jnp.float32)
        .astype(jnp.bfloat16)
        .reshape(requests, step_count, heads_local, head_dim)
    )
    key_new = (
        jnp.dot(scaled, w_key, preferred_element_type=jnp.float32)
        .astype(jnp.bfloat16)
        .reshape(requests, step_count, inner_local)
    )
    value_new = (
        jnp.dot(scaled, w_value, preferred_element_type=jnp.float32)
        .astype(jnp.bfloat16)
        .reshape(requests, step_count, inner_local)
    )
    position = seq_index * span_local + jnp.arange(span_local, dtype=jnp.int32)
    target = lengths[:, None] + jnp.arange(step_count, dtype=jnp.int32)[None, :]
    landing = position[None, None, :] == target[:, :, None]
    landed = jnp.any(landing, axis=1)[:, :, None]
    landing_low = landing.astype(jnp.bfloat16)
    placed_keys = jnp.einsum(
        "rtp,rtc->rpc", landing_low, key_new, preferred_element_type=jnp.float32
    ).astype(jnp.bfloat16)
    placed_values = jnp.einsum(
        "rtp,rtc->rpc", landing_low, value_new, preferred_element_type=jnp.float32
    ).astype(jnp.bfloat16)
    key_rows = jnp.where(landed, placed_keys, cache_keys).reshape(
        requests, span_local, heads_local, head_dim
    )
    value_rows = jnp.where(landed, placed_values, cache_values).reshape(
        requests, span_local, heads_local, head_dim
    )
    scores = jnp.einsum("rthd,rphd->rthp", queries, key_rows, preferred_element_type=jnp.float32)
    bucket_hot = (buckets[..., None] == jnp.arange(bucket_count, dtype=jnp.int32)).astype(
        jnp.float32
    )
    scores = scores + jnp.einsum(
        "rtpb,bh->rthp", bucket_hot, rel_bias, precision=lax.Precision.HIGHEST
    )
    allowed = (position[None, None, :] <= target[:, :, None])[:, :, None, :]
    scores = jnp.where(allowed, scores, -1e30)
    local_top = jnp.max(scores, axis=-1)
    weights = jnp.where(allowed, jnp.exp(scores - local_top[..., None]), 0.0)
    local_mass = jnp.sum(weights, axis=-1)
    partial_value = jnp.einsum(
        "rthp,rphd->rthd", weights, value_rows.astype(jnp.float32), precision=lax.Precision.HIGHEST
    )
    out_rows = w_out.astype(jnp.float32)
    global_top, global_mass, summed = joined(
        (local_top, local_mass, partial_value), "seq", join_three
    )
    heads_out = (summed / global_mass[..., None]).reshape(tokens, inner_local)
    projected = jnp.dot(heads_out, out_rows, precision=lax.Precision.HIGHEST)
    mixed_rows = lax.psum(projected, "head")
    hidden_one = states + mixed_rows
    normed, _ = norm_parts(hidden_one, ffn_gain)
    router_logits = jnp.dot(normed, w_router, precision=lax.Precision.HIGHEST)
    normed_low = normed.astype(jnp.bfloat16)
    expert_total = w_router.shape[1]
    local_experts, model_width, units_local = w_gate.shape
    expert_ids = jnp.arange(expert_total, dtype=jnp.int32)
    pick_marks = (expert_picks[..., None] == expert_ids).astype(jnp.int32)
    per_step = jnp.sum(pick_marks, axis=2)
    earlier = jnp.cumsum(per_step, axis=1) - per_step
    slot_index = jnp.sum(pick_marks * earlier[:, :, None, :], axis=-1)
    pick_total = expert_picks.shape[2]
    token_picks = jnp.transpose(expert_picks, (1, 0, 2)).reshape(tokens, pick_total)
    token_slots = jnp.transpose(slot_index, (1, 0, 2)).reshape(tokens, pick_total)
    token_steps = jnp.arange(tokens, dtype=jnp.int32) % step_count
    picked = jnp.sum(
        jnp.where(token_picks[..., None] == expert_ids, router_logits[:, None, :], 0.0), axis=-1
    )
    gate_first = jax.nn.sigmoid(picked[:, 0] - picked[:, 1])
    gate_second = jax.nn.sigmoid(picked[:, 1] - picked[:, 0])
    slot_rows = step_count * CAP
    row_ids = jnp.arange(local_experts * slot_rows, dtype=jnp.int32)
    row_expert = head_index * local_experts + row_ids // slot_rows
    row_step = row_ids // CAP % step_count
    row_slot = row_ids % CAP
    chooser = jnp.zeros((row_ids.shape[0], tokens), jnp.float32)
    for pick_rank in range(pick_total):
        matched = (
            (row_expert[:, None] == token_picks[None, :, pick_rank])
            & (row_step[:, None] == token_steps[None, :])
            & (row_slot[:, None] == token_slots[None, :, pick_rank])
        )
        chooser = chooser + matched.astype(jnp.float32)
    routed = jnp.dot(
        chooser.astype(jnp.bfloat16), normed_low, preferred_element_type=jnp.float32
    ).astype(jnp.bfloat16)
    routed = routed.reshape(local_experts, slot_rows, model_width)
    gate_part = jnp.einsum("esd,edf->esf", routed, w_gate, preferred_element_type=jnp.float32)
    up_part = jnp.einsum("esd,edf->esf", routed, w_up, preferred_element_type=jnp.float32)
    hidden_units = (jax.nn.gelu(gate_part, approximate=True) * up_part).astype(jnp.bfloat16)
    down_part = jnp.einsum("esf,efd->esd", hidden_units, w_down, preferred_element_type=jnp.float32)
    expert_share = lax.psum_scatter(down_part, "seq", scatter_dimension=2, tiled=True).astype(
        jnp.bfloat16
    )
    share_width = expert_share.shape[2]
    collected = lax.all_gather(expert_share[None], ("seq", "head"), axis=0, tiled=True)
    arranged = collected.reshape(seq_count, head_count, local_experts, slot_rows, share_width)
    arranged = jnp.transpose(arranged, (1, 2, 3, 0, 4)).reshape(
        expert_total * slot_rows, seq_count * share_width
    )
    group_size = tokens // head_count
    first_row = head_index * group_size
    own_picks = lax.dynamic_slice_in_dim(token_picks, first_row, group_size, 0)
    own_slots = lax.dynamic_slice_in_dim(token_slots, first_row, group_size, 0)
    own_steps = lax.dynamic_slice_in_dim(token_steps, first_row, group_size, 0)
    own_first = lax.dynamic_slice_in_dim(gate_first, first_row, group_size, 0)
    own_second = lax.dynamic_slice_in_dim(gate_second, first_row, group_size, 0)
    own_hidden = lax.dynamic_slice_in_dim(hidden_one, first_row, group_size, 0)
    flat_rows = own_picks * slot_rows + own_steps[:, None] * CAP + own_slots
    every_row = jnp.arange(expert_total * slot_rows, dtype=jnp.int32)
    select_first = (flat_rows[:, 0:1] == every_row[None, :]).astype(jnp.bfloat16)
    select_second = (flat_rows[:, 1:2] == every_row[None, :]).astype(jnp.bfloat16)
    expert_mix = own_first[:, None] * jnp.dot(
        select_first, arranged, preferred_element_type=jnp.float32
    )
    expert_mix = expert_mix + own_second[:, None] * jnp.dot(
        select_second, arranged, preferred_element_type=jnp.float32
    )
    final_rows = (own_hidden + expert_mix).astype(jnp.bfloat16)
    scaled_out, norm_root = norm_parts(final_rows.astype(jnp.float32), final_gain)
    logits = jnp.dot(scaled_out.astype(jnp.bfloat16), w_vocab, preferred_element_type=jnp.float32)
    top_logit = lax.pmax(jnp.max(logits, axis=-1), "seq")
    return (final_rows, norm_root, top_logit)


def solution(mesh):
    placed = (
        P(),
        P(),
        P(None, "seq", "head"),
        P(None, "seq", "head"),
        P(None, None, "seq"),
        P(),
        P(None, "head"),
        P(None, "head"),
        P(None, "head"),
        P(None, "head"),
        P("head", None),
        P(),
        P(),
        P("head", None, "seq"),
        P("head", None, "seq"),
        P("head", "seq", None),
        P(),
        P(),
        P(None, "seq"),
    )
    return jax.shard_map(
        shards,
        mesh=mesh,
        in_specs=placed,
        out_specs=(P("head", None), P("head"), P("head")),
        check_vma=False,
    )
```

profile of v0, /device:TPU:32, one launch (start us, length us, event | category | flops | bytes accessed | tf_op | source)
XLA Modules:
  0.0 482.6 jit_solution(6117893066806250847)
XLA Ops:
  7.3 1.2 fusion.13
  9.2 1.3 convolution_convert_fusion.2
  10.7 1.3 convolution_convert_fusion.1
  12.3 4.6 copy.74
  17.0 4.7 copy.77
  22.0 2.0 fusion.4
  24.0 3.1 convert_select_fusion.1
  27.1 1.0 convert_select_fusion
  28.8 3.3 convolution_bitcast_fusion.1
  33.2 25.3 %all-gather.1 = f32[768,4,2]{1,2,0:T(2,128)S(1)} all-gather(f32[24,4,2]{1,2,0:T(2,128)S(1)} %fusion.16), channel_id=3, replica_groups=mesh['seq'=32,'head'=8] {'seq'}, dimensions={0}, use_global_device_ids=true | all-gather | bytes 25344 | tf_op jit(solution)/shard_map/all_gather | solution.py:10
  59.2 25.2 %all-gather = f32[768,4,2]{1,2,0:T(2,128)S(1)} all-gather(f32[24,4,2]{1,2,0:T(2,128)S(1)} %get-tuple-element.240), channel_id=2, replica_groups=mesh['seq'=32,'head'=8] {'seq'}, dimensions={0}, use_global_device_ids=true | all-gather | bytes 25344 | tf_op jit(solution)/shard_map/all_gather | solution.py:10
  84.4 1.2 copy.83
  87.0 76.0 %while.19 = (s32[]{:T(128)}, f32[24,4,2]{0,2,1:T(2,128)S(1)}, f32[24,4,2]{0,2,1:T(2,128)S(1)}, f32[24,4,2,64]{3,2,1,0:T(2,128)S(1)}, f32[32,24,4,2]{1,3,2,0:T(2,...) while((s32[]{:T(128)}, f32[24,4,2]{0,2,1:T(2,128)S(1)}, ...), condition=%wide.region_5.6_spmd, body=%wide.region_4.5_spmd.sunk | while | flops 38021 | bytes 256655 | solution.py:15
  90.4 0.9 constant_dynamic-slice_fusion.6
  92.8 0.9 constant_dynamic-slice_fusion.6
  95.3 0.9 constant_dynamic-slice_fusion.6
  97.7 0.9 constant_dynamic-slice_fusion.6
  119.8 0.9 constant_dynamic-slice_fusion.6
  122.3 0.9 constant_dynamic-slice_fusion.6
  124.7 0.9 constant_dynamic-slice_fusion.6
  163.4 1.1 fusion.77
  164.6 72.5 %all-reduce.2.cloned.1.call-done = f32[96,1024]{1,0:T(8,128)} async-done(((f32[96,1024]{1,0:T(8,128)}), f32[96,1024]{1,0:T(8,128)}) %all-reduce.2.cloned.1.call-update) | async-done | bytes 393232 | tf_op jit(solution)/shard_map/psum | solution.py:120
  237.1 1.1 multiply_reduce_fusion
  239.1 1.2 fusion.78
  240.3 2.0 fusion.12
  242.3 1.3 copy.98
  243.6 1.4 reshape.208
  245.2 83.7 %reduce-scatter.4.cloned.1.call-done = f32[32,32]{1,0:T(8,128)} async-done(((f32[1024,32]{1,0:T(8,128)}), f32[32,32]{1,0:T(8,128)}) %reduce-scatter.4.cloned.1.call-update) | async-done | bytes 4112
  329.8 73.4 %all-gather.3 = bf16[512,16,32]{2,1,0:T(8,128)(2,1)S(1)} all-gather(bf16[2,16,32]{2,1,0:T(8,128)(2,1)S(1)} %copy.99), channel_id=5, replica_groups=mesh['seq'=32,'head'=8] {'seq','head'}, dimensions={0}, use_global_device_ids=true | all-gather | bytes 526336 | tf_op jit(solution)/shard_map/all_gather | solution.py:166
  403.2 2.7 copy.112
  405.9 3.5 reshape.189
  410.8 65.3 %pmax.7 = f32[12]{0:T(128)} all-reduce(f32[12]{0:T(128)S(1)} %convolution_reduce_fusion), channel_id=1, replica_groups=mesh['seq'=32,'head'=8] {'seq'}, use_global_device_ids=true, to_apply=%region_15.16 | all-reduce | flops 12 | bytes 96 | tf_op jit(solution)/shard_map/pmax | solution.py:192
  (233 shorter events, 78.1 us)
Async XLA Ops:
  7.2 402.9 %copy-start = (bf16[1024,1004]{0,1:T(8,128)(2,1)S(1)}, bf16[1024,1004]{0,1:T(8,128)(2,1)}, u32[]{:S(2)}) copy-start(bf16[1024,1004]{0,1:T(8,128)(2,1)} %param.39) | copy-start | bytes 6168580
  7.2 4.8 copy-start.2
  7.2 4.8 copy-start.12
  7.2 4.8 copy-start.9
  7.2 78.8 %all-gather.6.cloned.1.call-start = ((), (), s32[]{:S(2)}) async-start(), calls=%async_computation.2 | async-start | bytes 3244032 | tf_op jit(solution)/shard_map/all_gather | solution.py:10
  16.9 5.0 %copy-start.10 = (s32[24,4,512]{2,1,0:T(4,128)S(1)}, s32[24,4,512]{2,1,0:T(4,128)}, u32[]{:S(2)}) copy-start(s32[24,4,512]{2,1,0:T(4,128)} %param.25) | copy-start | bytes 589828
  17.0 5.0 %copy-start.14 = (f32[32,2]{0,1:T(2,128)S(1)}, f32[32,2]{0,1:T(2,128)}, u32[]{:S(2)}) copy-start(f32[32,2]{0,1:T(2,128)} %param.30) | copy-start | bytes 772
  24.0 3.1 copy-start.1
  28.8 3.3 copy-start.6
  32.1 205.0 %all-reduce.2.cloned.1.call-start = ((), (), s32[]{:S(2)}) async-start(), calls=%async_computation.1 | async-start | bytes 786432 | tf_op jit(solution)/shard_map/psum | solution.py:120
  59.1 104.3 %copy-start.4 = (bf16[128,1024]{1,0:T(8,128)(2,1)S(1)}, bf16[128,1024]{1,0:T(8,128)(2,1)}, u32[]{:S(2)}) copy-start(bf16[128,1024]{1,0:T(8,128)(2,1)} %param.31) | copy-start | bytes 786436
  86.9 151.3 %copy-start.11 = (f32[1024,16]{0,1:T(8,128)S(1)}, f32[1024,16]{0,1:T(8,128)}, u32[]{:S(2)}) copy-start(f32[1024,16]{0,1:T(8,128)} %param.33) | copy-start | bytes 196612
  87.0 151.3 %copy-start.13 = (f32[1024]{0:T(1024)S(1)}, f32[1024]{0:T(1024)}, u32[]{:S(2)}) copy-start(f32[1024]{0:T(1024)} %param.32) | copy-start | bytes 12292
  163.0 77.3 %copy-start.3 = (bf16[2,88,1024]{2,1,0:T(8,128)(2,1)S(1)}, bf16[2,88,1024]{2,1,0:T(8,128)(2,1)}, u32[]{:S(2)}) copy-start(bf16[2,88,1024]{2,1,0:T(8,128)(2,1)} %param.36) | copy-start | bytes 1081348
  164.5 164.3 %reduce-scatter.4.cloned.1.call-start = ((), (), s32[]{:S(2)}) async-start(), calls=%async_computation.3 | async-start | bytes 540672
  403.2 6.8 %copy-start.7 = (f32[1024]{0:T(1024)S(1)}, f32[1024]{0:T(1024)}, u32[]{:S(2)}) copy-start(f32[1024]{0:T(1024)} %param.38) | copy-start | bytes 12292
  410.0 66.1 %copy-start.5 = (bf16[12,1024]{1,0:T(8,128)(2,1)}, bf16[12,1024]{1,0:T(8,128)(2,1)S(1)}, u32[]{:S(2)}) copy-start(bf16[12,1024]{1,0:T(8,128)(2,1)S(1)} %get-tuple-element.243) | copy-start | bytes 73732
  410.0 66.1 %copy-start.8 = (f32[12]{0:T(128)}, f32[12]{0:T(128)S(1)}, u32[]{:S(2)}) copy-start(f32[12]{0:T(128)S(1)} %add_sqrt_fusion) | copy-start | bytes 148
Sparse Core Ops, SparseCore 0:
  32.2 53.7 all-gather.5
  164.6 72.4 all-reduce.1
  245.2 83.6 reduce-scatter.3
where the time goes:
time: 485 us; the launch traced here: 483 us
  blocking collectives  189 us (39%)
  waiting for transfers between devices  156 us (32%)
  local copies, waits for them, and re-layouts  58.1 us (12%)
  other arithmetic  44.9 us (9%)
  matrix products  19.3 us (4%)
  between operations  14.1 us (3%)
    unnamed x4, waiting for transfers between devices  83.7 us
    all_gather x1, blocking collectives, shards(): lax.all_gather(expert_share[None], ('seq', 'head'), axis=0, tiled=True)  73.4 us
    psum x1, waiting for transfers between devices, shards(): mixed_rows = lax.psum(projected, 'head')  72.5 us
    pmax x1, blocking collectives, shards(): top_logit = lax.pmax(jnp.max(logits, axis=-1), 'seq')  65.3 us
    all_gather x2, blocking collectives, joined(): gathered = jax.tree.map(lambda a: lax.all_gather(a, axis), part)  50.5 us
    dynamic_slice x34, local copies, waits for them, and re-layouts, take(): lax.dynamic_index_in_dim(a, source, 0, False)  28.9 us
    add x31, other arithmetic, join_three(): mass = earlier_part[1] * lead_scale + later_part[1] * trail_scale  21.9 us
    add x31, other arithmetic, join_three(): earlier_part[2] * lead_scale[..., None]  18.8 us
  transfers between devices with their start and end apart: 3, of which 3 were waited for; matrix products, arithmetic and copies ran while one was open for 1% of the time, Pallas kernels for 0%

commit v1 on v0

--- a/solution.py
+++ b/solution.py
@@ -117,7 +117,7 @@
     )
     heads_out = (summed / global_mass[..., None]).reshape(tokens, inner_local)
     projected = jnp.dot(heads_out, out_rows, precision=lax.Precision.HIGHEST)
-    mixed_rows = lax.psum(projected, "head")
+    mixed_rows = jnp.sum(lax.all_gather(projected, "head"), axis=0)
     hidden_one = states + mixed_rows
     normed, _ = norm_parts(hidden_one, ffn_gain)
     router_logits = jnp.dot(normed, w_router, precision=lax.Precision.HIGHEST)

time: 485 us -> 458 us (0.944)
  waiting for transfers between devices: 156 us -> 128 us
    psum x1 -> x0, waiting for transfers between devices: 72.5 us -> none  [shards(): mixed_rows = lax.psum(projected, 'head')]
    all_gather x0 -> x1, waiting for transfers between devices: none -> 42.8 us  [shards(): mixed_rows = jnp.sum(lax.all_gather(projected, 'head'), axis=0)]
where the time goes in v1:
time: 458 us; the launch traced here: 455 us
  blocking collectives  189 us (41%)
  waiting for transfers between devices  128 us (28%)
  local copies, waits for them, and re-layouts  58.1 us (13%)
  other arithmetic  46.1 us (10%)
  matrix products  19.1 us (4%)
  between operations  14.1 us (3%)
    unnamed x4, waiting for transfers between devices  84.3 us
    all_gather x1, blocking collectives, shards(): lax.all_gather(expert_share[None], ('seq', 'head'), axis=0, tiled=True)  73.4 us
    pmax x1, blocking collectives, shards(): top_logit = lax.pmax(jnp.max(logits, axis=-1), 'seq')  65.3 us
    all_gather x2, blocking collectives, joined(): gathered = jax.tree.map(lambda a: lax.all_gather(a, axis), part)  50.3 us
    all_gather x1, waiting for transfers between devices, shards(): mixed_rows = jnp.sum(lax.all_gather(projected, 'head'), axis=0)  42.8 us
    dynamic_slice x34, local copies, waits for them, and re-layouts, take(): lax.dynamic_index_in_dim(a, source, 0, False)  28.9 us
    add x31, other arithmetic, join_three(): mass = earlier_part[1] * lead_scale + later_part[1] * trail_scale  21.9 us
    add x31, other arithmetic, join_three(): earlier_part[2] * lead_scale[..., None]  18.8 us
  transfers between devices with their start and end apart: 3, of which 3 were waited for; matrix products, arithmetic and copies ran while one was open for 1% of the time, Pallas kernels for 0%

profile of v1, /device:TPU:32, one launch (start us, length us, event | category | flops | bytes accessed | tf_op | source)
XLA Modules:
  0.0 455.0 jit_solution(17341566296934083669)
XLA Ops:
  7.3 1.2 fusion.13
  9.2 1.3 convolution_convert_fusion.2
  10.7 1.3 convolution_convert_fusion.1
  12.3 4.6 %copy.74 = bf16[24,512,128]{1,2,0:T(8,128)(2,1)} copy(bf16[24,512,128]{2,1,0:T(8,128)(2,1)} %param.23) | data formatting | bytes 6291456 | tf_op args[2]
  17.0 4.7 %copy.77 = bf16[24,512,128]{1,2,0:T(8,128)(2,1)} copy(bf16[24,512,128]{2,1,0:T(8,128)(2,1)} %param.24) | data formatting | bytes 6291456 | tf_op args[3]
  22.0 2.0 fusion.4
  24.0 3.1 convert_select_fusion.1
  27.1 1.0 convert_select_fusion
  28.8 3.3 convolution_bitcast_fusion.1
  32.5 25.2 %all-gather.1 = f32[768,4,2]{1,2,0:T(2,128)S(1)} all-gather(f32[24,4,2]{1,2,0:T(2,128)S(1)} %fusion.16), channel_id=3, replica_groups=mesh['seq'=32,'head'=8] {'seq'}, dimensions={0}, use_global_device_ids=true | all-gather | bytes 25344 | tf_op jit(solution)/shard_map/all_gather | solution.py:10
  58.4 25.1 %all-gather = f32[768,4,2]{1,2,0:T(2,128)S(1)} all-gather(f32[24,4,2]{1,2,0:T(2,128)S(1)} %get-tuple-element.240), channel_id=2, replica_groups=mesh['seq'=32,'head'=8] {'seq'}, dimensions={0}, use_global_device_ids=true | all-gather | bytes 25344 | tf_op jit(solution)/shard_map/all_gather | solution.py:10
  83.6 1.2 copy.83
  86.6 76.0 %while.19 = (s32[]{:T(128)}, f32[24,4,2]{0,2,1:T(2,128)S(1)}, f32[24,4,2]{0,2,1:T(2,128)S(1)}, f32[24,4,2,64]{3,2,1,0:T(2,128)S(1)}, f32[32,24,4,2]{1,3,2,0:T(2,...) while((s32[]{:T(128)}, f32[24,4,2]{0,2,1:T(2,128)S(1)}, ...), condition=%wide.region_5.6_spmd, body=%wide.region_4.5_spmd.sunk | while | flops 38021 | bytes 256655 | solution.py:15
  87.5 0.9 constant_dynamic-slice_fusion.6
  104.7 0.9 constant_dynamic-slice_fusion.6
  117.0 0.9 constant_dynamic-slice_fusion.6
  136.6 0.9 constant_dynamic-slice_fusion.6
  141.5 0.9 constant_dynamic-slice_fusion.6
  144.0 0.9 constant_dynamic-slice_fusion.6
  148.9 0.9 constant_dynamic-slice_fusion.6
  163.1 1.1 fusion.77
  165.1 42.8 %all-gather.10.cloned.1.call-done = f32[768,1024]{1,0:T(8,128)} async-done(((f32[96,1024]{1,0:T(8,128)}), f32[768,1024]{1,0:T(8,128)}) %all-gather.10.cloned.1.call-update) | async-done | bytes 3145744 | tf_op jit(solution)/shard_map/all_gather | solution.py:120
  207.9 2.2 reduce_sum.74
  210.2 1.3 fusion.31
  212.1 2.0 fusion.12
  214.1 1.3 copy.98
  215.4 1.4 reshape.209
  217.0 84.2 %reduce-scatter.4.cloned.1.call-done = f32[32,32]{1,0:T(8,128)} async-done(((f32[1024,32]{1,0:T(8,128)}), f32[32,32]{1,0:T(8,128)}) %reduce-scatter.4.cloned.1.call-update) | async-done | bytes 4112
  302.1 73.4 %all-gather.4 = bf16[512,16,32]{2,1,0:T(8,128)(2,1)S(1)} all-gather(bf16[2,16,32]{2,1,0:T(8,128)(2,1)S(1)} %copy.99), channel_id=6, replica_groups=mesh['seq'=32,'head'=8] {'seq','head'}, dimensions={0}, use_global_device_ids=true | all-gather | bytes 526336 | tf_op jit(solution)/shard_map/all_gather | solution.py:166
  375.6 2.7 copy.112
  378.3 3.5 reshape.189
  383.2 65.3 %pmax.7 = f32[12]{0:T(128)} all-reduce(f32[12]{0:T(128)S(1)} %convolution_reduce_fusion), channel_id=1, replica_groups=mesh['seq'=32,'head'=8] {'seq'}, use_global_device_ids=true, to_apply=%region_15.16 | all-reduce | flops 12 | bytes 96 | tf_op jit(solution)/shard_map/pmax | solution.py:192
  (234 shorter events, 78.6 us)
Async XLA Ops:
  7.2 375.2 %copy-start = (bf16[1024,1004]{0,1:T(8,128)(2,1)S(1)}, bf16[1024,1004]{0,1:T(8,128)(2,1)}, u32[]{:S(2)}) copy-start(bf16[1024,1004]{0,1:T(8,128)(2,1)} %param.39) | copy-start | bytes 6168580
  7.2 4.8 %copy-start.2 = (bf16[96,1024]{1,0:T(8,128)(2,1)S(1)}, bf16[96,1024]{1,0:T(8,128)(2,1)}, u32[]{:S(2)}) copy-start(bf16[96,1024]{1,0:T(8,128)(2,1)} %param.21) | copy-start | bytes 589828
  7.2 4.8 %copy-start.12 = (f32[1024]{0:T(1024)S(1)}, f32[1024]{0:T(1024)}, u32[]{:S(2)}) copy-start(f32[1024]{0:T(1024)} %param.26) | copy-start | bytes 12292
  7.2 4.8 %copy-start.10 = (bf16[1024,128]{1,0:T(8,128)(2,1)S(1)}, bf16[1024,128]{1,0:T(8,128)(2,1)}, u32[]{:S(2)}) copy-start(bf16[1024,128]{1,0:T(8,128)(2,1)} %param.28) | copy-start | bytes 786436
  7.2 78.4 %all-gather.8.cloned.1.call-start = ((), (), s32[]{:S(2)}) async-start(), calls=%async_computation.1 | async-start | bytes 3244032 | tf_op jit(solution)/shard_map/all_gather | solution.py:10
  16.9 5.0 %copy-start.11 = (s32[24,4,512]{2,1,0:T(4,128)S(1)}, s32[24,4,512]{2,1,0:T(4,128)}, u32[]{:S(2)}) copy-start(s32[24,4,512]{2,1,0:T(4,128)} %param.25) | copy-start | bytes 589828
  17.0 5.0 %copy-start.14 = (f32[32,2]{0,1:T(2,128)S(1)}, f32[32,2]{0,1:T(2,128)}, u32[]{:S(2)}) copy-start(f32[32,2]{0,1:T(2,128)} %param.30) | copy-start | bytes 772
  24.0 3.1 copy-start.1
  32.1 175.8 %all-gather.10.cloned.1.call-start = ((), (), s32[]{:S(2)}) async-start(), calls=%async_computation.2 | async-start | bytes 3538944 | tf_op jit(solution)/shard_map/all_gather | solution.py:120
  58.4 104.7 %copy-start.5 = (bf16[128,1024]{1,0:T(8,128)(2,1)S(1)}, bf16[128,1024]{1,0:T(8,128)(2,1)}, u32[]{:S(2)}) copy-start(bf16[128,1024]{1,0:T(8,128)(2,1)} %param.31) | copy-start | bytes 786436
  84.8 79.4 %copy-start.7 = (s32[4,24,2]{1,2,0:T(2,128)S(1)}, s32[4,24,2]{1,2,0:T(2,128)}, u32[]{:S(2)}) copy-start(s32[4,24,2]{1,2,0:T(2,128)} %param.37) | copy-start | bytes 2308
  163.0 47.2 %copy-start.13 = (f32[1024]{0:T(1024)S(1)}, f32[1024]{0:T(1024)}, u32[]{:S(2)}) copy-start(f32[1024]{0:T(1024)} %param.32) | copy-start | bytes 12292
  164.1 137.1 %reduce-scatter.4.cloned.1.call-start = ((), (), s32[]{:S(2)}) async-start(), calls=%async_computation.3 | async-start | bytes 540672
  207.9 4.2 copy-start.3
  210.1 1.8 copy-start.4
  375.6 6.8 %copy-start.8 = (f32[1024]{0:T(1024)S(1)}, f32[1024]{0:T(1024)}, u32[]{:S(2)}) copy-start(f32[1024]{0:T(1024)} %param.38) | copy-start | bytes 12292
  382.4 66.1 %copy-start.6 = (bf16[12,1024]{1,0:T(8,128)(2,1)}, bf16[12,1024]{1,0:T(8,128)(2,1)S(1)}, u32[]{:S(2)}) copy-start(bf16[12,1024]{1,0:T(8,128)(2,1)S(1)} %get-tuple-element.243) | copy-start | bytes 73732
  382.4 66.1 %copy-start.9 = (f32[12]{0:T(128)}, f32[12]{0:T(128)S(1)}, u32[]{:S(2)}) copy-start(f32[12]{0:T(128)S(1)} %add_sqrt_fusion) | copy-start | bytes 148
Sparse Core Ops, SparseCore 0:
  32.2 53.4 all-gather.7
  164.3 43.5 all-gather.9
  217.0 84.2 reduce-scatter.3
